TPU v7x, 32 devices: a whole 2x2x4 slice. The times are simulated.
32 devices in a mesh: groups: 2 (over y), aa: 4 (over z), ba: 4 (over x, core).
Axes of the slice: x: 2, y: 2, z: 4, core: 2. Of those that a mesh axis runs over, the one named last changes fastest.
Arguments:
- alignment_state: bfloat16 [64, 128, 256], P(('groups', 'aa'), 'ba'), parts along dimension 0, may hold values from -1.5 to 1.5
- pair_state: bfloat16 [256, 128, 128], P(('groups', 'aa'), 'ba'), parts along dimension 0, may hold values from -1.796875 to 1.796875
- alignment_mask: int32 [64, 128], P(('groups', 'aa'), 'ba'), parts along dimension 0, may hold values from 0 to 1, as said below
- left_weight: bfloat16 [256, 32], replicated, may hold values from -0.375 to 0.375
- right_weight: bfloat16 [256, 32], replicated, may hold values from -0.375 to 0.375
- outer_output_weight: bfloat16 [1024, 128], replicated, may hold values from -0.75 to 0.75
- pair_bias_weight: bfloat16 [128, 8], replicated, may hold values from -40 to 40
- query_weight: bfloat16 [256, 256], replicated, may hold values from -0.375 to 0.375
- key_weight: bfloat16 [256, 256], replicated, may hold values from -0.375 to 0.375
- value_weight: bfloat16 [256, 256], replicated, may hold values from -0.375 to 0.375
- gate_weight: bfloat16 [256, 256], replicated, may hold values from -0.375 to 0.375
- output_weight: bfloat16 [256, 256], replicated, may hold values from -1.5 to 1.5
- up_weight: bfloat16 [256, 1024], replicated, may hold values from -0.375 to 0.375
- down_weight: bfloat16 [1024, 256], replicated, may hold values from -0.1875 to 0.1875
Outputs:
- alignment_output: bfloat16 [64, 128, 256], P(('groups', 'aa'), 'ba'), parts along dimension 0
- pair_output: bfloat16 [256, 128, 128], P(('groups', 'aa'), 'ba'), parts along dimension 0
There are 2 independent parts, one for each index of `groups`. A program takes and returns all parts, laid end to end along the dimension named above; an argument that names none is the same for every part. Nothing has to cross between parts.
Inputs may be any that keep to these rules, and one draw needn't show every extreme that they name: `alignment_mask`: every residue of the first sequence is kept (mask 1); other entries are kept at random.
All inputs are finite; a program needn't handle non-finite values.
Results may differ from a plain program's by a relative error of at most 0.013.
The roundings to bfloat16 on the way count: a program that leaves them out, or rounds other values in their place, can miss the bound.
Values may be sent and summed in bfloat16 or wider, within the bound.
No kernel may reach another device: no remote copies, remote signals or barrier semaphores. Data moves between devices by JAX's collectives and lax.ppermute only.
A program may use at most 128 MiB of HBM per device.

v0:
```python
import jax
import jax.numpy as jnp
from jax import lax
from jax.sharding import PartitionSpec as P


def from_root(x, axis, root):
    mine = lax.axis_index(axis) == root
    return lax.psum(jnp.where(mine, x, jnp.zeros_like(x)), axis)


def row_norm_input(values):
    center = values - jnp.mean(values, axis=-1, keepdims=True)
    spread = jnp.mean(center * center, axis=-1, keepdims=True)
    return center * lax.rsqrt(spread + 1e-05)


def attend_block(carried, query_all, key_piece, value_piece, valid_piece, bias_part):
    top_old, mass_old, accum_old = carried
    scores = (
        jnp.einsum("sihd,sjhd->shij", query_all, key_piece, preferred_element_type=jnp.float32)
        + bias_part[None]
    )
    scores = jnp.where(valid_piece[:, None, None, :] > 0, scores, -1000000000.0)
    new_top = jnp.maximum(top_old, jnp.max(scores, axis=-1))
    weights_raw = jnp.exp(scores - new_top[:, :, :, None])
    mass_new = jnp.sum(weights_raw, axis=-1)
    accum_new = jnp.einsum(
        "shij,sjhd->shid",
        weights_raw.astype(jnp.bfloat16),
        value_piece,
        preferred_element_type=jnp.float32,
    )
    return (new_top, mass_new, accum_new)


def per_device(
    alignment_state,
    pair_state,
    alignment_mask,
    left_weight,
    right_weight,
    outer_output_weight,
    pair_bias_weight,
    query_weight,
    key_weight,
    value_weight,
    gate_weight,
    output_weight,
    up_weight,
    down_weight,
):
    sequence_count, residue_count, channel_count = alignment_state.shape
    opm_width = left_weight.shape[1]
    num_heads = pair_bias_weight.shape[1]
    head_width = query_weight.shape[1] // num_heads
    layer_normed = row_norm_input(alignment_state.astype(jnp.float32)).astype(jnp.bfloat16)
    flat_rows = layer_normed.reshape(sequence_count * residue_count, channel_count)
    row_keep_mask = alignment_mask.astype(jnp.float32)
    keep_half = row_keep_mask.astype(jnp.bfloat16)
    left_fac = (
        jnp.dot(flat_rows, left_weight, preferred_element_type=jnp.float32).reshape(
            sequence_count, residue_count, opm_width
        )
        * row_keep_mask[:, :, None]
    ).astype(jnp.bfloat16)
    right_fac = (
        jnp.dot(flat_rows, right_weight, preferred_element_type=jnp.float32).reshape(
            sequence_count, residue_count, opm_width
        )
        * row_keep_mask[:, :, None]
    ).astype(jnp.bfloat16)
    col_left, col_right, col_keep = (
        lax.all_gather(left_fac, "aa", axis=0, tiled=True),
        lax.all_gather(right_fac, "aa", axis=0, tiled=True),
        lax.all_gather(keep_half, "aa", axis=0, tiled=True),
    )
    row_left, row_keep = (
        from_root(col_left, "ba", lax.axis_index("aa")),
        from_root(col_keep, "ba", lax.axis_index("aa")),
    )
    seq_total = col_right.shape[0]
    pair_count = jnp.dot(row_keep.T, col_keep, preferred_element_type=jnp.float32)
    left_flat = row_left.reshape(seq_total, residue_count * opm_width)
    right_flat = col_right.reshape(seq_total, residue_count * opm_width)
    row_block = 8

    def outer_block(block_index):
        left_part = lax.dynamic_slice_in_dim(
            left_flat, block_index * (row_block * opm_width), row_block * opm_width, 1
        )
        outer_sum = lax.dot_general(
            left_part, right_flat, (((0,), (0,)), ((), ())), preferred_element_type=jnp.float32
        )
        outer_sum = outer_sum.reshape(row_block, opm_width, residue_count, opm_width).transpose(
            0, 2, 1, 3
        )
        outer_sum = outer_sum.reshape(row_block * residue_count, opm_width * opm_width).astype(
            jnp.bfloat16
        )
        return jnp.dot(outer_sum, outer_output_weight, preferred_element_type=jnp.float32).reshape(
            row_block, residue_count, -1
        )

    update = lax.map(outer_block, jnp.arange(residue_count // row_block, dtype=jnp.int32)).reshape(
        residue_count, residue_count, -1
    )
    pair_output = (pair_state.astype(jnp.float32) + update / pair_count[:, :, None]).astype(
        jnp.bfloat16
    )
    pair_normed = row_norm_input(pair_output.astype(jnp.float32)).astype(jnp.bfloat16)
    tile_bias = jnp.dot(
        pair_normed.reshape(residue_count * residue_count, -1),
        pair_bias_weight,
        preferred_element_type=jnp.float32,
    )
    tile_bias = tile_bias.reshape(residue_count, residue_count, num_heads).transpose(2, 0, 1)
    rows_bias = lax.all_gather(tile_bias, "ba", axis=2, tiled=True)
    bias_here = from_root(rows_bias, "aa", lax.axis_index("ba"))
    score_scale = head_width ** (-0.5)
    query_all = (
        (jnp.dot(flat_rows, query_weight, preferred_element_type=jnp.float32) * score_scale)
        .astype(jnp.bfloat16)
        .reshape(sequence_count, residue_count, num_heads, head_width)
    )
    gate_act = jax.nn.sigmoid(jnp.dot(flat_rows, gate_weight, preferred_element_type=jnp.float32))
    start_state = (
        jnp.full((sequence_count, num_heads, residue_count), -1e30, jnp.float32),
        jnp.zeros((sequence_count, num_heads, residue_count), jnp.float32),
        jnp.zeros((sequence_count, num_heads, residue_count, head_width), jnp.float32),
    )
    w_pair = jnp.concatenate((key_weight, value_weight), axis=1)
    rows_in = lax.all_gather(layer_normed, "ba", axis=1, tiled=True)
    valid_piece = lax.all_gather(keep_half, "ba", axis=1, tiled=True)
    span_len = rows_in.shape[1]
    key_value = jnp.dot(
        rows_in.reshape(sequence_count * span_len, channel_count),
        w_pair,
        preferred_element_type=jnp.float32,
    ).astype(jnp.bfloat16)
    key_value = key_value.reshape(sequence_count, span_len, 2, num_heads, head_width)
    final_state = attend_block(
        start_state, query_all, key_value[:, :, 0], key_value[:, :, 1], valid_piece, bias_here
    )
    attended = final_state[2] / final_state[1][:, :, :, None]
    attended = attended.transpose(0, 2, 1, 3).reshape(
        sequence_count * residue_count, num_heads * head_width
    )
    gated_row_output = (attended * gate_act).astype(jnp.bfloat16)
    alignment_middle = alignment_state.astype(jnp.float32) + jnp.dot(
        gated_row_output, output_weight, preferred_element_type=jnp.float32
    ).reshape(sequence_count, residue_count, channel_count)
    middle_normed = (
        row_norm_input(alignment_middle)
        .astype(jnp.bfloat16)
        .reshape(sequence_count * residue_count, channel_count)
    )
    hidden_units = jax.nn.relu(
        jnp.dot(middle_normed, up_weight, preferred_element_type=jnp.float32)
    ).astype(jnp.bfloat16)
    alignment_output = (
        alignment_middle
        + jnp.dot(hidden_units, down_weight, preferred_element_type=jnp.float32).reshape(
            sequence_count, residue_count, channel_count
        )
    ).astype(jnp.bfloat16)
    return (alignment_output, pair_output)


def solution(mesh):
    return jax.shard_map(
        per_device,
        mesh=mesh,
        in_specs=(
            P(("groups", "aa"), "ba", None),
            P(("groups", "aa"), "ba", None),
            P(("groups", "aa"), "ba"),
            P(),
            P(),
            P(),
            P(),
            P(),
            P(),
            P(),
            P(),
            P(),
            P(),
            P(),
        ),
        out_specs=(P(("groups", "aa"), "ba", None), P(("groups", "aa"), "ba", None)),
        check_vma=False,
    )
```

profile of v0, /device:TPU:0, one launch (start us, length us, event | category | flops | bytes accessed | tf_op | source)
XLA Modules:
  0.0 188.1 jit_solution(4134955716603868108)
XLA Ops:
  7.3 1.1 convert_reduce_fusion.1
  8.4 1.1 fusion.30
  9.5 1.0 fusion.31
  10.5 0.7 convert_convert_fusion
  11.2 0.9 fusion.15
  12.1 15.7 %all_gather.20 = bf16[32,32,32]{2,1,0:T(8,128)(2,1)S(1)} all-gather(bf16[8,32,32]{2,1,0:T(8,128)(2,1)S(1)} %fusion.15), channel_id=1, replica_groups=mesh['groups'=2,'aa'=4,'ba'=4] {'aa'}, dimensions={0}, use_global_device_ids=true | all-gather | bytes 81920 | tf_op jit(solution)/shard_map/all_gather | solution.py:74
  27.8 0.9 reshape.112
  28.8 7.2 %all_gather.19 = bf16[8,128,256]{2,1,0:T(8,128)(2,1)S(1)} all-gather(bf16[8,32,256]{2,1,0:T(8,128)(2,1)S(1)} %fusion.31), channel_id=1, replica_groups=mesh['groups'=2,'aa'=4,'ba'=4] {'ba'}, dimensions={1}, use_global_device_ids=true | all-gather | bytes 655360 | tf_op jit(solution)/shard_map/all_gather | solution.py:133
  36.1 12.0 %all_gather.22 = bf16[32,32]{1,0:T(8,128)(2,1)S(1)} all-gather(bf16[8,32]{1,0:T(8,128)(2,1)S(1)} %get-tuple-element.49), channel_id=1, replica_groups=mesh['groups'=2,'aa'=4,'ba'=4] {'aa'}, dimensions={0}, use_global_device_ids=true | all-gather | bytes 2560 | tf_op jit(solution)/shard_map/all_gather | solution.py:76
  48.1 5.8 %psum.22 = bf16[32,32]{1,0:T(8,128)(2,1)S(1)} all-reduce(bf16[32,32]{1,0:T(8,128)(2,1)S(1)} %broadcast_select_fusion.2), channel_id=1, replica_groups=mesh['groups'=2,'aa'=4,'ba'=4] {'ba'}, use_global_device_ids=true, to_apply=%region_5.6 | all-reduce | flops 1024 | bytes 4096 | tf_op jit(solution)/shard_map/psum | solution.py:9
  55.2 1.1 fusion.46
  56.6 13.9 %all_gather.21 = bf16[32,32,32]{2,1,0:T(8,128)(2,1)S(1)} all-gather(bf16[8,32,32]{2,1,0:T(8,128)(2,1)S(1)} %fusion.16), channel_id=1, replica_groups=mesh['groups'=2,'aa'=4,'ba'=4] {'aa'}, dimensions={0}, use_global_device_ids=true | all-gather | bytes 81920 | tf_op jit(solution)/shard_map/all_gather | solution.py:75
  70.5 0.9 reshape.113
  71.4 1.0 reshape.109
  72.4 5.6 %all-gather = bf16[4,32,8]{1,2,0:T(8,128)(2,1)} all-gather(bf16[1,32,8]{1,2,0:T(8,128)(2,1)S(1)} %bitcast.97), channel_id=1, replica_groups=mesh['groups'=2,'aa'=4,'ba'=4] {'ba'}, dimensions={0}, use_global_device_ids=true | all-gather | bytes 2560 | tf_op jit(solution)/shard_map/all_gather | solution.py:134
  78.6 45.7 %while.10 = (s32[]{:T(128)}, f32[4,8,32,128]{3,2,1,0:T(8,128)}, s32[4]{0:T(128)}, bf16[32,1024]{1,0:T(8,128)(2,1)}, bf16[32,1024]{1,0:T(8,128)(2,1)}, /*index=5*...) while((s32[]{:T(128)}, f32[4,8,32,128]{3,2,1,0:T(8,128)}, s32[4]{0:T(128)}, ...), condition=%wide.region_4.5_spmd, body=%wide.region_3.4_spmd.sunk | while | flops 84148224 | bytes 4670115 | solution.py:105
  78.6 1.3 dynamic_slice.12
  80.6 1.2 convolution_convert_fusion.3
  81.8 1.6 convert_element_type.141
  83.4 2.2 %copy.52 = bf16[8,32,32,32]{3,2,1,0:T(8,128)(2,1)} copy(bf16[8,32,32,32]{3,1,2,0:T(8,128)(2,1)S(1)} %bitcast.86) | data formatting | bytes 1048576 | tf_op jit(solution)/shard_map/while/body/eval_jaxpr/convert_element_type | solution.py:98
  85.5 3.5 %convert_element_type.142 = bf16[8,32,1024]{2,1,0:T(8,128)(2,1)S(1)} reshape(bf16[8,32,32,32]{3,2,1,0:T(8,128)(2,1)} %copy.52) | data formatting | bytes 1048576 | tf_op jit(solution)/shard_map/while/body/eval_jaxpr/convert_element_type | solution.py:98
  89.1 0.9 fusion.73
  90.0 1.3 dynamic_slice.12
  92.0 1.2 convolution_convert_fusion.3
  93.2 1.6 convert_element_type.141
  94.8 2.2 %copy.52 = bf16[8,32,32,32]{3,2,1,0:T(8,128)(2,1)} copy(bf16[8,32,32,32]{3,1,2,0:T(8,128)(2,1)S(1)} %bitcast.86) | data formatting | bytes 1048576 | tf_op jit(solution)/shard_map/while/body/eval_jaxpr/convert_element_type | solution.py:98
  96.9 3.5 %convert_element_type.142 = bf16[8,32,1024]{2,1,0:T(8,128)(2,1)S(1)} reshape(bf16[8,32,32,32]{3,2,1,0:T(8,128)(2,1)} %copy.52) | data formatting | bytes 1048576 | tf_op jit(solution)/shard_map/while/body/eval_jaxpr/convert_element_type | solution.py:98
  100.5 0.9 fusion.73
  101.4 1.3 dynamic_slice.12
  103.4 1.2 convolution_convert_fusion.3
  104.6 1.6 convert_element_type.141
  106.2 2.2 %copy.52 = bf16[8,32,32,32]{3,2,1,0:T(8,128)(2,1)} copy(bf16[8,32,32,32]{3,1,2,0:T(8,128)(2,1)S(1)} %bitcast.86) | data formatting | bytes 1048576 | tf_op jit(solution)/shard_map/while/body/eval_jaxpr/convert_element_type | solution.py:98
  108.4 3.5 %convert_element_type.142 = bf16[8,32,1024]{2,1,0:T(8,128)(2,1)S(1)} reshape(bf16[8,32,32,32]{3,2,1,0:T(8,128)(2,1)} %copy.52) | data formatting | bytes 1048576 | tf_op jit(solution)/shard_map/while/body/eval_jaxpr/convert_element_type | solution.py:98
  111.9 0.9 fusion.73
  112.8 1.3 dynamic_slice.12
  114.8 1.2 convolution_convert_fusion.3
  116.0 1.6 convert_element_type.141
  117.6 2.2 %copy.52 = bf16[8,32,32,32]{3,2,1,0:T(8,128)(2,1)} copy(bf16[8,32,32,32]{3,1,2,0:T(8,128)(2,1)S(1)} %bitcast.86) | data formatting | bytes 1048576 | tf_op jit(solution)/shard_map/while/body/eval_jaxpr/convert_element_type | solution.py:98
  119.8 3.5 %convert_element_type.142 = bf16[8,32,1024]{2,1,0:T(8,128)(2,1)S(1)} reshape(bf16[8,32,32,32]{3,2,1,0:T(8,128)(2,1)} %copy.52) | data formatting | bytes 1048576 | tf_op jit(solution)/shard_map/while/body/eval_jaxpr/convert_element_type | solution.py:98
  123.3 1.0 fusion.73
  124.3 1.3 fusion.24
  126.3 1.2 convolution_bitcast_fusion.2
  127.6 7.3 %all_gather.23 = f32[8,32,128]{1,0,2:T(8,128)S(1)} all-gather(f32[8,32,32]{1,0,2:T(8,128)S(1)} %copy.34), channel_id=1, replica_groups=mesh['groups'=2,'aa'=4,'ba'=4] {'ba'}, dimensions={2}, use_global_device_ids=true | all-gather | bytes 163840 | tf_op jit(solution)/shard_map/all_gather | solution.py:118
  134.9 0.8 broadcast_select_fusion
  135.9 38.8 %all-reduce.5.cloned.1.call-done = f32[8,32,128]{1,0,2:T(8,128)} async-done(((f32[8,32,128]{1,0,2:T(8,128)}), f32[8,32,128]{1,0,2:T(8,128)}) %all-reduce.5.cloned.1.call-update) | async-done | bytes 131088 | tf_op jit(solution)/shard_map/psum | solution.py:9
  174.6 1.2 copy.35
  177.1 1.1 fusion.4
  180.6 0.7 add_convert_fusion
  (67 shorter events, 6.7 us)
Async XLA Ops:
  7.2 172.8 %copy-start = (bf16[1024,256]{1,0:T(8,128)(2,1)S(1)}, bf16[1024,256]{1,0:T(8,128)(2,1)}, u32[]{:S(2)}) copy-start(bf16[1024,256]{1,0:T(8,128)(2,1)} %param.29) | copy-start | bytes 1572868
  7.2 28.8 %copy-start.11 = (bf16[256,32]{0,1:T(8,128)(2,1)S(1)}, bf16[256,32]{0,1:T(8,128)(2,1)}, u32[]{:S(2)}) copy-start(bf16[256,32]{0,1:T(8,128)(2,1)} %param.20) | copy-start | bytes 49156
  7.2 46.7 %copy-start.8 = (bf16[256,256]{1,0:T(8,128)(2,1)S(1)}, bf16[256,256]{1,0:T(8,128)(2,1)}, u32[]{:S(2)}) copy-start(bf16[256,256]{1,0:T(8,128)(2,1)} %param.24) | copy-start | bytes 393220
  7.2 46.7 %copy-start.7 = (bf16[256,256]{1,0:T(8,128)(2,1)S(1)}, bf16[256,256]{1,0:T(8,128)(2,1)}, u32[]{:S(2)}) copy-start(bf16[256,256]{1,0:T(8,128)(2,1)} %param.25) | copy-start | bytes 393220
  7.2 70.8 %all-reduce.3.cloned.1.call-start = ((), (), s32[]{:S(2)}) async-start(), calls=%async_computation | async-start | bytes 131072 | tf_op jit(solution)/shard_map/psum | solution.py:9
  28.7 145.9 %all-reduce.5.cloned.1.call-start = ((), (), s32[]{:S(2)}) async-start(), calls=%async_computation.1 | async-start | bytes 1048576 | tf_op jit(solution)/shard_map/psum | solution.py:9
  54.9 1.4 copy-start.9
  55.2 23.4 %copy-start.1 = (bf16[1024,128]{1,0:T(8,128)(2,1)S(1)}, bf16[1024,128]{1,0:T(8,128)(2,1)}, u32[]{:S(2)}) copy-start(bf16[1024,128]{1,0:T(8,128)(2,1)} %param.21) | copy-start | bytes 786436
  125.6 50.3 %copy-start.3 = (bf16[32,32,128]{2,1,0:T(8,128)(2,1)}, bf16[32,32,128]{2,1,0:T(8,128)(2,1)S(1)}, u32[]{:S(2)}) copy-start(bf16[32,32,128]{2,1,0:T(8,128)(2,1)S(1)} %fusion.24) | copy-start | bytes 786436
  125.6 10.1 %copy-start.10 = (bf16[4,32,8]{1,2,0:T(8,128)(2,1)S(1)}, bf16[4,32,8]{1,2,0:T(8,128)(2,1)}, u32[]{:S(2)}) copy-start(bf16[4,32,8]{1,2,0:T(8,128)(2,1)} %all-gather) | copy-start | bytes 6148
  125.8 50.0 %copy-start.4 = (bf16[8,32,8,32]{3,2,1,0:T(8,128)(2,1)S(1)}, bf16[8,32,8,32]{3,2,1,0:T(8,128)(2,1)}, u32[]{:S(2)}) copy-start(bf16[8,32,8,32]{3,2,1,0:T(8,128)(2,1)} %reshape.109) | copy-start | bytes 393220
  125.8 50.0 %copy-start.6 = (bf16[8,128,1,8,32]{1,0,4,3,2:T(8,128)(2,1)S(1)}, bf16[8,128,1,8,32]{1,0,4,3,2:T(8,128)(2,1)}, u32[]{:S(2)}) copy-start(bf16[8,128,1,8,32]{1,0,4,3,2:T(8,128)(2,1)} %get-tuple-element.48) | copy-start | bytes 1572868
  135.9 41.2 %copy-start.5 = (bf16[8,128,1,8,32]{1,0,4,3,2:T(8,128)(2,1)S(1)}, bf16[8,128,1,8,32]{1,0,4,3,2:T(8,128)(2,1)}, u32[]{:S(2)}) copy-start(bf16[8,128,1,8,32]{1,0,4,3,2:T(8,128)(2,1)} %get-tuple-element.47) | copy-start | bytes 1572868
  178.2 1.0 copy-start.13
  178.2 1.0 copy-start.14
  178.2 1.3 copy-start.2
  178.8 1.2 copy-start.12
Sparse Core Ops, SparseCore 0:
  28.9 33.0 all-reduce.2
  135.9 38.7 all-reduce.4
where the time goes:
time: 189 us; the launch traced here: 188 us
  blocking collectives  67.4 us (36%)
  local copies, waits for them, and re-layouts  42 us (22%)
  waiting for transfers between devices  38.8 us (21%)
  between operations  14.5 us (8%)
  matrix products  14 us (7%)
  other arithmetic  8.53 us (5%)
  loops' own time  2.9 us (2%)
    psum x2, waiting for transfers between devices, from_root(): return lax.psum(jnp.where(mine, x, jnp.zeros_like(x)), axis)  38.8 us
    convert_element_type x12, local copies, waits for them, and re-layouts, outer_block(): outer_sum.reshape(row_block * residue_count, opm_width * opm_width)  29.1 us
    all_gather x1, blocking collectives, per_device(): lax.all_gather(left_fac, 'aa', axis=0, tiled=True)  15.7 us
    all_gather x1, blocking collectives, per_device(): lax.all_gather(right_fac, 'aa', axis=0, tiled=True)  13.9 us
    all_gather x1, blocking collectives, per_device(): lax.all_gather(keep_half, 'aa', axis=0, tiled=True)  12 us
    all_gather x1, blocking collectives, per_device(): rows_bias = lax.all_gather(tile_bias, 'ba', axis=2, tiled=True)  7.28 us
    all_gather x1, blocking collectives, per_device(): rows_in = lax.all_gather(layer_normed, 'ba', axis=1, tiled=True)  7.17 us
    psum x1, blocking collectives, from_root(): return lax.psum(jnp.where(mine, x, jnp.zeros_like(x)), axis)  5.76 us
  transfers between devices with their start and end apart: 2, of which 1 were waited for; matrix products, arithmetic and copies ran while one was open for 3% of the time, Pallas kernels for 0%

commit v1 on v0

--- a/solution.py
+++ b/solution.py
@@ -6,7 +6,7 @@
 
 def from_root(x, axis, root):
     mine = lax.axis_index(axis) == root
-    return lax.psum(jnp.where(mine, x, jnp.zeros_like(x)), axis)
+    return jnp.sum(lax.all_gather(jnp.where(mine, x, jnp.zeros_like(x)), axis), axis=0)
 
 
 def row_norm_input(values):

time: 189 us -> 178 us (0.942)
  blocking collectives: 67.4 us -> 115 us
  waiting for transfers between devices: 38.8 us -> 0 us
  between operations: 14.5 us -> 0.99 us
  local copies, waits for them, and re-layouts: 42 us -> 36.6 us
    all_gather x0 -> x3, blocking collectives: none -> 53.6 us  [from_root(): lax.all_gather(jnp.where(mine, x, jnp.zeros_like(x)), axis)]
    psum x2 -> x0, waiting for transfers between devices: 38.8 us -> none  [from_root(): return lax.psum(jnp.where(mine, x, jnp.zeros_like(x)), axis)]
    psum x1 -> x0, blocking collectives: 5.76 us -> none  [from_root(): return lax.psum(jnp.where(mine, x, jnp.zeros_like(x)), axis)]
    dynamic_slice x4, local copies, waits for them, and re-layouts: 5.27 us -> 2.65 us  [per_device(): lax.map(outer_block, jnp.arange(residue_count // row_block, dtype=jnp.int...]
  transfers between devices with their start and end apart: 2 -> 0, of which waited for: 1 -> 0; matrix products, arithmetic and copies ran while one was open for 3% -> 0% of each run, Pallas kernels for 0% -> 0%
where the time goes in v1:
time: 178 us; the launch traced here: 177 us
  blocking collectives  115 us (65%)
  local copies, waits for them, and re-layouts  36.6 us (21%)
  matrix products  13.3 us (7%)
  other arithmetic  8.38 us (5%)
  loops' own time  2.9 us (2%)
    all_gather x3, blocking collectives, from_root(): lax.all_gather(jnp.where(mine, x, jnp.zeros_like(x)), axis)  53.6 us
    convert_element_type x12, local copies, waits for them, and re-layouts, outer_block(): outer_sum.reshape(row_block * residue_count, opm_width * opm_width)  29.1 us
    all_gather x1, blocking collectives, per_device(): lax.all_gather(left_fac, 'aa', axis=0, tiled=True)  15.7 us
    all_gather x1, blocking collectives, per_device(): lax.all_gather(right_fac, 'aa', axis=0, tiled=True)  14.3 us
    all_gather x1, blocking collectives, per_device(): lax.all_gather(keep_half, 'aa', axis=0, tiled=True)  12.2 us
    all_gather x1, blocking collectives, per_device(): rows_bias = lax.all_gather(tile_bias, 'ba', axis=2, tiled=True)  7.28 us
    all_gather x1, blocking collectives, per_device(): rows_in = lax.all_gather(layer_normed, 'ba', axis=1, tiled=True)  6.51 us
    all_gather x1, blocking collectives, per_device(): valid_piece = lax.all_gather(keep_half, 'ba', axis=1, tiled=True)  5.37 us

profile of v1, /device:TPU:0, one launch (start us, length us, event | category | flops | bytes accessed | tf_op | source)
XLA Modules:
  0.0 177.2 jit_solution(13666760070082602428)
XLA Ops:
  0.6 1.1 convert_reduce_fusion.1
  1.7 1.1 fusion.30
  2.9 1.0 fusion.31
  3.9 0.7 convert_convert_fusion
  4.6 0.9 fusion.15
  5.5 15.7 %all_gather.38 = bf16[32,32,32]{2,1,0:T(8,128)(2,1)S(1)} all-gather(bf16[8,32,32]{2,1,0:T(8,128)(2,1)S(1)} %fusion.15), channel_id=1, replica_groups=mesh['groups'=2,'aa'=4,'ba'=4] {'aa'}, dimensions={0}, use_global_device_ids=true | all-gather | bytes 81920 | tf_op jit(solution)/shard_map/all_gather | solution.py:74
  21.2 10.2 %all-gather = bf16[128,32,32]{2,1,0:T(8,128)(2,1)S(1)} all-gather(bf16[32,32,32]{2,1,0:T(8,128)(2,1)S(1)} %broadcast_select_fusion.1), channel_id=2, replica_groups=mesh['groups'=2,'aa'=4,'ba'=4] {'ba'}, dimensions={0}, use_global_device_ids=true | all-gather | bytes 327680 | tf_op jit(solution)/shard_map/all_gather | solution.py:9
  31.6 0.9 reshape.112
  32.7 14.3 %all_gather.41 = bf16[32,32,32]{2,1,0:T(8,128)(2,1)S(1)} all-gather(bf16[8,32,32]{2,1,0:T(8,128)(2,1)S(1)} %fusion.16), channel_id=1, replica_groups=mesh['groups'=2,'aa'=4,'ba'=4] {'aa'}, dimensions={0}, use_global_device_ids=true | all-gather | bytes 81920 | tf_op jit(solution)/shard_map/all_gather | solution.py:75
  47.0 0.9 reshape.113
  47.9 43.1 %while.10 = (s32[]{:T(128)}, f32[4,8,32,128]{3,2,1,0:T(8,128)}, s32[4]{0:T(128)S(1)}, bf16[32,1024]{1,0:T(8,128)(2,1)}, bf16[32,1024]{1,0:T(8,128)(2,1)}, /*inde...) while((s32[]{:T(128)}, f32[4,8,32,128]{3,2,1,0:T(8,128)}, ...), condition=%wide.region_4.5_spmd, body=%wide.region_3.4_spmd.sunk | while | flops 84148224 | bytes 4670115 | solution.py:105
  48.0 0.7 dynamic_slice.12
  49.3 1.2 convolution_convert_fusion.3
  50.5 1.6 convert_element_type.145
  52.1 2.2 %copy.53 = bf16[8,32,32,32]{3,2,1,0:T(8,128)(2,1)} copy(bf16[8,32,32,32]{3,1,2,0:T(8,128)(2,1)S(1)} %bitcast.90) | data formatting | bytes 1048576 | tf_op jit(solution)/shard_map/while/body/eval_jaxpr/convert_element_type | solution.py:98
  54.3 3.5 %convert_element_type.146 = bf16[8,32,1024]{2,1,0:T(8,128)(2,1)S(1)} reshape(bf16[8,32,32,32]{3,2,1,0:T(8,128)(2,1)} %copy.53) | data formatting | bytes 1048576 | tf_op jit(solution)/shard_map/while/body/eval_jaxpr/convert_element_type | solution.py:98
  57.8 0.9 fusion.73
  58.7 0.7 dynamic_slice.12
  60.1 1.2 convolution_convert_fusion.3
  61.3 1.6 convert_element_type.145
  62.9 2.2 %copy.53 = bf16[8,32,32,32]{3,2,1,0:T(8,128)(2,1)} copy(bf16[8,32,32,32]{3,1,2,0:T(8,128)(2,1)S(1)} %bitcast.90) | data formatting | bytes 1048576 | tf_op jit(solution)/shard_map/while/body/eval_jaxpr/convert_element_type | solution.py:98
  65.0 3.5 %convert_element_type.146 = bf16[8,32,1024]{2,1,0:T(8,128)(2,1)S(1)} reshape(bf16[8,32,32,32]{3,2,1,0:T(8,128)(2,1)} %copy.53) | data formatting | bytes 1048576 | tf_op jit(solution)/shard_map/while/body/eval_jaxpr/convert_element_type | solution.py:98
  68.6 0.9 fusion.73
  69.5 0.7 dynamic_slice.12
  70.9 1.2 convolution_convert_fusion.3
  72.1 1.6 convert_element_type.145
  73.6 2.2 %copy.53 = bf16[8,32,32,32]{3,2,1,0:T(8,128)(2,1)} copy(bf16[8,32,32,32]{3,1,2,0:T(8,128)(2,1)S(1)} %bitcast.90) | data formatting | bytes 1048576 | tf_op jit(solution)/shard_map/while/body/eval_jaxpr/convert_element_type | solution.py:98
  75.8 3.5 %convert_element_type.146 = bf16[8,32,1024]{2,1,0:T(8,128)(2,1)S(1)} reshape(bf16[8,32,32,32]{3,2,1,0:T(8,128)(2,1)} %copy.53) | data formatting | bytes 1048576 | tf_op jit(solution)/shard_map/while/body/eval_jaxpr/convert_element_type | solution.py:98
  79.3 0.9 fusion.73
  80.3 0.7 dynamic_slice.12
  81.6 1.2 convolution_convert_fusion.3
  82.8 1.6 convert_element_type.145
  84.4 2.2 %copy.53 = bf16[8,32,32,32]{3,2,1,0:T(8,128)(2,1)} copy(bf16[8,32,32,32]{3,1,2,0:T(8,128)(2,1)S(1)} %bitcast.90) | data formatting | bytes 1048576 | tf_op jit(solution)/shard_map/while/body/eval_jaxpr/convert_element_type | solution.py:98
  86.6 3.5 %convert_element_type.146 = bf16[8,32,1024]{2,1,0:T(8,128)(2,1)S(1)} reshape(bf16[8,32,32,32]{3,2,1,0:T(8,128)(2,1)} %copy.53) | data formatting | bytes 1048576 | tf_op jit(solution)/shard_map/while/body/eval_jaxpr/convert_element_type | solution.py:98
  90.1 0.9 fusion.73
  91.1 12.2 %all_gather.42 = bf16[32,32]{1,0:T(8,128)(2,1)S(1)} all-gather(bf16[8,32]{1,0:T(8,128)(2,1)S(1)} %get-tuple-element.49), channel_id=1, replica_groups=mesh['groups'=2,'aa'=4,'ba'=4] {'aa'}, dimensions={0}, use_global_device_ids=true | all-gather | bytes 2560 | tf_op jit(solution)/shard_map/all_gather | solution.py:76
  103.3 5.2 %all-gather.1 = bf16[128,32]{1,0:T(8,128)(2,1)S(1)} all-gather(bf16[32,32]{1,0:T(8,128)(2,1)S(1)} %broadcast_select_fusion.2), channel_id=3, replica_groups=mesh['groups'=2,'aa'=4,'ba'=4] {'ba'}, dimensions={0}, use_global_device_ids=true | all-gather | bytes 10240 | tf_op jit(solution)/shard_map/all_gather | solution.py:9
  108.6 1.3 fusion.24
  111.3 7.3 %all_gather.45 = f32[8,32,128]{1,0,2:T(8,128)S(1)} all-gather(f32[8,32,32]{1,0,2:T(8,128)S(1)} %copy.32), channel_id=1, replica_groups=mesh['groups'=2,'aa'=4,'ba'=4] {'ba'}, dimensions={2}, use_global_device_ids=true | all-gather | bytes 163840 | tf_op jit(solution)/shard_map/all_gather | solution.py:118
  118.6 38.3 %all-gather.2 = f32[32,32,128]{1,0,2:T(8,128)S(1)} all-gather(f32[8,32,128]{1,0,2:T(8,128)S(1)} %broadcast_select_fusion), channel_id=4, replica_groups=mesh['groups'=2,'aa'=4,'ba'=4] {'aa'}, dimensions={0}, use_global_device_ids=true | all-gather | bytes 655360 | tf_op jit(solution)/shard_map/all_gather | solution.py:9
  157.4 6.5 %all_gather.37 = bf16[8,128,256]{2,1,0:T(8,128)(2,1)S(1)} all-gather(bf16[8,32,256]{2,1,0:T(8,128)(2,1)S(1)} %fusion.31), channel_id=1, replica_groups=mesh['groups'=2,'aa'=4,'ba'=4] {'ba'}, dimensions={1}, use_global_device_ids=true | all-gather | bytes 655360 | tf_op jit(solution)/shard_map/all_gather | solution.py:133
  164.4 0.5 copy.29
  166.3 5.4 %all-gather.3 = bf16[4,32,8]{1,2,0:T(8,128)(2,1)S(1)} all-gather(bf16[1,32,8]{1,2,0:T(8,128)(2,1)S(1)} %bitcast.103), channel_id=1, replica_groups=mesh['groups'=2,'aa'=4,'ba'=4] {'ba'}, dimensions={0}, use_global_device_ids=true | all-gather | bytes 2560 | tf_op jit(solution)/shard_map/all_gather | solution.py:134
  172.3 0.7 fusion.17
  172.9 1.1 fusion.4
  174.1 0.6 copy.36
  175.9 0.5 fusion.7
  176.5 0.7 add_convert_fusion
  (60 shorter events, 6.0 us)
Async XLA Ops:
  0.6 175.3 %copy-start = (bf16[1024,256]{1,0:T(8,128)(2,1)S(1)}, bf16[1024,256]{1,0:T(8,128)(2,1)}, u32[]{:S(2)}) copy-start(bf16[1024,256]{1,0:T(8,128)(2,1)} %param.29) | copy-start | bytes 1572868
  2.8 29.7 %copy-start.7 = (bf16[256,32]{0,1:T(8,128)(2,1)S(1)}, bf16[256,32]{0,1:T(8,128)(2,1)}, u32[]{:S(2)}) copy-start(bf16[256,32]{0,1:T(8,128)(2,1)} %param.20) | copy-start | bytes 49156
  21.1 26.8 %copy-start.1 = (bf16[1024,128]{1,0:T(8,128)(2,1)S(1)}, bf16[1024,128]{1,0:T(8,128)(2,1)}, u32[]{:S(2)}) copy-start(bf16[1024,128]{1,0:T(8,128)(2,1)} %param.21) | copy-start | bytes 786436
  47.9 62.6 %copy-start.11 = (bf16[128,8]{0,1:T(8,128)(2,1)S(1)}, bf16[128,8]{0,1:T(8,128)(2,1)}, u32[]{:S(2)}) copy-start(bf16[128,8]{0,1:T(8,128)(2,1)} %param.22) | copy-start | bytes 6148
  110.0 46.9 %copy-start.3 = (bf16[32,32,128]{2,1,0:T(8,128)(2,1)}, bf16[32,32,128]{2,1,0:T(8,128)(2,1)S(1)}, u32[]{:S(2)}) copy-start(bf16[32,32,128]{2,1,0:T(8,128)(2,1)S(1)} %fusion.24) | copy-start | bytes 786436
  156.9 7.1 %copy-start.4 = (bf16[256,256]{1,0:T(8,128)(2,1)S(1)}, bf16[256,256]{1,0:T(8,128)(2,1)}, u32[]{:S(2)}) copy-start(bf16[256,256]{1,0:T(8,128)(2,1)} %param.25) | copy-start | bytes 393220
  156.9 7.1 %copy-start.5 = (bf16[256,256]{1,0:T(8,128)(2,1)S(1)}, bf16[256,256]{1,0:T(8,128)(2,1)}, u32[]{:S(2)}) copy-start(bf16[256,256]{1,0:T(8,128)(2,1)} %param.24) | copy-start | bytes 393220
  164.9 0.9 copy-start.6
  174.1 1.0 copy-start.9
  174.1 1.0 copy-start.10
  174.1 1.3 copy-start.2
  174.7 1.2 copy-start.8
